TPU v7x, 512 devices: a whole 4x4x16 slice. The times are simulated.
512 devices in a mesh: test: 8 (over z_lo, core), bx: 4 (over y), by: 16 (over z_hi, x).
Axes of the slice: x: 4, y: 4, z: 16 (z_hi: 4, z_lo: 4; z = z_hi * 4 + z_lo), core: 2. Of those that a mesh axis runs over, the one named last changes fastest.
Arguments:
- log_conductivity: float32 [32, 128, 256], P('bx', 'by'), may hold values from -3 to 3
- storage: float32 [32, 128, 256], P('bx', 'by'), may hold values from 0.5 to 2
- recharge: float32 [32, 128, 256], P('bx', 'by'), may hold values from -6 to 6
- pump_rate: float32 [32], P('test'), may hold values from 4 to 16
- pump_well: int32 [32], P('test'), may hold values from 0 to 2047
- observed: float32 [32, 2048], P('test'), may hold values from -9 to 9
- owner: int32 [2048], replicated, may hold values from 0 to 63, as said below
- screen_column: int32 [2048], replicated, may hold values from 0 to 63
- screen_top: int32 [2048], replicated, may hold values from 0 to 248
Outputs:
- gradient: float32 [32, 128, 256], P('bx', 'by', 'test')
Inputs may be any that keep to these rules, and one draw needn't show every extreme that they name: `owner`: each brick owns exactly 32 wells.
All inputs are finite; a program needn't handle non-finite values.
Results may differ from a plain program's by a relative error of at most 0.0001.
Values sent between devices are 32-bit elements; how exact they have to be, the bound alone decides.
A program may use at most 64 MiB of HBM per device.

v0:
```python
import jax
import jax.numpy as jnp
from jax import lax
from jax.sharding import PartitionSpec as P

SWEEPS = 3
SCREEN = 8
epsilon = 1e-06


def with_halo(block, sides, width):
    for axis, dim in sides:
        count = lax.axis_size(axis)
        forward = [(i, i + 1) for i in range(count - 1)]
        backward = [(target, source) for source, target in forward]
        low = lax.ppermute(
            lax.slice_in_dim(block, block.shape[dim] - width, None, axis=dim), axis, forward
        )
        high = lax.ppermute(lax.slice_in_dim(block, 0, width, axis=dim), axis, backward)
        block = jnp.concatenate([low, block, high], axis=dim)
    return block


def pad_depth(values):
    return jnp.pad(values, [(0, 0)] * (values.ndim - 1) + [(1, 1)])


def neighbours(padded, centre):
    z_padded = pad_depth(centre)
    return [
        padded[..., 2:, 1:-1, :],
        padded[..., :-2, 1:-1, :],
        padded[..., 1:-1, 2:, :],
        padded[..., 1:-1, :-2, :],
        z_padded[..., 2:],
        z_padded[..., :-2],
    ]


def weighted(conductance, others):
    accumulated = conductance[0] * others[0]
    for position in range(1, 6):
        accumulated = accumulated + conductance[position] * others[position]
    return accumulated


def sensitivity(conductance, heads_field, heads_padded, adjoint_field, adjoint_padded):
    near_heads = neighbours(heads_padded, heads_field)
    near_adjoint = neighbours(adjoint_padded, adjoint_field)
    accumulated = jnp.zeros_like(heads_field)
    for position in range(6):
        accumulated = accumulated + conductance[position] * (heads_field - near_heads[position]) * (
            adjoint_field - near_adjoint[position]
        )
    return -0.5 * accumulated


def relax_field(source, conductance, diagonal):
    iterate = source / diagonal
    for sweep_index in range(SWEEPS - 1):
        padded = with_halo(iterate, (("bx", 1), ("by", 2)), 1)
        iterate = (source + weighted(conductance, neighbours(padded, iterate))) / diagonal
    return iterate


def per_sweep_terms(
    log_conductivity,
    storage,
    recharge,
    pump_rate,
    pump_well,
    observed,
    owner,
    screen_column,
    screen_top,
):
    size_x, size_y, size_z = log_conductivity.shape
    tests_here = pump_rate.shape[0]
    cell_count = size_x * size_y * size_z
    padded_log = with_halo(log_conductivity, (("bx", 0), ("by", 1)), 1)
    conductance = [
        jnp.exp(0.5 * (log_conductivity + other))
        for other in neighbours(padded_log, log_conductivity)
    ]
    diagonal = storage + weighted(conductance, [1.0] * 6)
    brick_index = lax.axis_index("bx") * lax.axis_size("by") + lax.axis_index("by")
    offsets = jnp.arange(SCREEN, dtype=jnp.int32)
    screen_cells = (screen_column * size_z + screen_top)[:, None] + offsets[None, :]
    owned_here = owner == brick_index
    pump_cells = screen_cells[pump_well]
    pump_value = jnp.where(owner[pump_well] == brick_index, -pump_rate, 0.0)
    test_rows = jnp.arange(tests_here, dtype=jnp.int32)[:, None]
    flat_source = jnp.broadcast_to(recharge.reshape(1, cell_count), (tests_here, cell_count))
    flat_source = flat_source.at[test_rows, pump_cells].add(
        jnp.broadcast_to(pump_value[:, None], pump_cells.shape)
    )
    source = flat_source.reshape(tests_here, size_x, size_y, size_z)
    heads_field = relax_field(source, conductance, diagonal)
    well_heads = jnp.mean(heads_field.reshape(tests_here, cell_count)[:, screen_cells], axis=2)
    residual = jnp.where(owned_here[None, :], well_heads - observed, 0.0)
    well_count = residual.shape[1]
    misfit = lax.psum(jnp.sum(residual * residual, axis=1), ("bx", "by")) / well_count + epsilon
    weights = residual / misfit[:, None]
    values = jnp.broadcast_to(weights[:, :, None], (tests_here, well_count, SCREEN)).reshape(
        tests_here, -1
    )
    adjoint_source = (
        jnp.zeros((tests_here, cell_count), jnp.float32).at[:, screen_cells.reshape(-1)].add(values)
    )
    adjoint_field = relax_field(
        adjoint_source.reshape(tests_here, size_x, size_y, size_z), conductance, diagonal
    )
    stacked = with_halo(
        jnp.concatenate([heads_field, adjoint_field], axis=0), (("bx", 1), ("by", 2)), 1
    )
    test_terms = sensitivity(
        conductance, heads_field, stacked[:tests_here], adjoint_field, stacked[tests_here:]
    )
    return (test_terms, misfit)


def local(
    log_conductivity,
    storage,
    recharge,
    pump_rate,
    pump_well,
    observed,
    owner,
    screen_column,
    screen_top,
):
    size_z = log_conductivity.shape[2]
    tests_here = pump_rate.shape[0]
    test_terms, misfit = per_sweep_terms(
        log_conductivity,
        storage,
        recharge,
        pump_rate,
        pump_well,
        observed,
        owner,
        screen_column,
        screen_top,
    )
    local_sum = jnp.sum(test_terms, axis=0)
    all_tests = tests_here * lax.axis_size("test")
    grand_total = lax.psum(local_sum, "test")
    slab_depth = size_z // lax.axis_size("test")
    gradient = lax.dynamic_slice_in_dim(
        grand_total, lax.axis_index("test") * slab_depth, slab_depth, 2
    )
    return gradient / all_tests


def solution(mesh):
    placed = (
        P("bx", "by", None),
        P("bx", "by", None),
        P("bx", "by", None),
        P("test"),
        P("test"),
        P("test", None),
        P(),
        P(),
        P(),
    )
    return jax.shard_map(
        local, mesh=mesh, in_specs=placed, out_specs=P("bx", "by", "test"), check_vma=False
    )
```

profile of v0, /device:TPU:2, one launch (start us, length us, event | category | flops | bytes accessed | tf_op | source)
XLA Modules:
  0.0 626.8 jit_solution(6473687219000279522)
XLA Ops:
  7.3 3.5 collective-permute-start.1
  10.7 1.3 collective-permute-start
  14.3 1.3 gather_fusion.1
  16.6 5.6 collective-permute-start.2
  22.2 1.9 collective-permute-start.3
  25.0 0.9 copy.25
  26.0 2.1 scatter_fusion
  28.1 1.2 add_add_fusion
  29.5 1.3 collective-permute-start.4
  30.8 5.2 collective-permute-start.5
  36.0 1.6 collective-permute-done.5
  37.6 3.9 collective-permute-start.6
  41.5 1.9 collective-permute-start.7
  44.3 3.1 collective-permute-done.7
  48.0 1.1 fusion.9
  49.1 1.3 collective-permute-start.8
  50.4 4.9 collective-permute-start.9
  55.3 1.5 collective-permute-done.9
  56.9 1.9 collective-permute-start.10
  58.8 4.6 collective-permute-start.11
  64.0 1.1 copy.21
  65.4 4.7 copy.20
  70.1 58.2 %gather_fusion.2 = f32[16384,4]{1,0:T(8,128)} fusion(f32[4,16384]{0,1:T(8,128)} %bitcast.34, s32[16384]{0:T(1024)S(1)} %broadcast_clamp_fusion), kind=kCustom, calls=%fused_computation.2 | custom fusion | bytes 589824 | tf_op jit(solution)/shard_map/gather | solution.py:99
  128.3 13.0 %bitcast_reduce_fusion = f32[2048,4]{1,0:T(8,128)S(1)} fusion(f32[16384,4]{1,0:T(8,128)} %gather_fusion.2), kind=kLoop, calls=%fused_computation.7 | loop fusion | flops 57344 | bytes 294912 | tf_op jit(solution)/shard_map/reduce_sum | solution.py:99
  142.5 236.4 %psum.14 = f32[4]{0:T(128)S(1)} all-reduce(f32[4]{0:T(128)S(1)} %multiply_reduce_fusion), channel_id=1, replica_groups=mesh['test'=8,'bx'=4,'by'=16] {'bx','by'}, use_global_device_ids=true, to_apply=%region_3.4 | all-reduce | flops 4 | bytes 32 | tf_op jit(solution)/shard_map/psum | solution.py:102
  379.4 91.6 %scatter_custom_fusion.1 = f32[4,16384]{0,1:T(8,128)} fusion(s32[16384]{0:T(1024)} %bitcast.41, f32[4,2048]{0,1:T(8,128)S(1)} %broadcast_divide_fusion, f32[]{:T(128)} %constant.27.clone.1), kind=kCustom, calls=%fused_computation.5 | custom fusion | flops 65536 | bytes 295424 | tf_op jit(solution)/shard_map/scatter-add | solution.py:108
  471.0 5.2 copy.24
  476.3 1.3 collective-permute-start.12
  477.6 4.5 collective-permute-start.13
  482.1 1.6 collective-permute-done.13
  483.8 4.0 collective-permute-start.14
  487.8 1.9 collective-permute-start.15
  489.7 4.0 collective-permute-done.15
  493.9 1.3 collective-permute-start.16
  495.2 4.9 collective-permute-start.17
  500.1 1.6 collective-permute-done.17
  501.7 1.9 collective-permute-start.18
  503.7 3.9 collective-permute-start.19
  507.6 1.9 collective-permute-done.19
  509.8 1.3 collective-permute-start.20
  511.1 4.9 collective-permute-start.21
  516.3 1.6 collective-permute-done.21
  518.0 1.9 collective-permute-start.22
  519.9 3.9 collective-permute-start.23
  524.3 1.9 collective-permute-done.23
  526.2 1.1 fusion.35
  527.4 91.2 %all-reduce.9.cloned.1.call-done = f32[8,8,256]{2,1,0:T(8,128)} async-done(((f32[8,8,256]{2,1,0:T(8,128)}), f32[8,8,256]{2,1,0:T(8,128)}) %all-reduce.9.cloned.1.call-update) | async-done | bytes 65552 | tf_op jit(solution)/shard_map/psum | solution.py:148
  618.5 1.4 dynamic-slice_multiply_fusion
  (83 shorter events, 10.5 us)
Async XLA Ops:
  6.5 56.9 %copy-start = (s32[2048]{0:T(1024)S(1)}, s32[2048]{0:T(1024)}, u32[]{:S(2)}) copy-start(s32[2048]{0:T(1024)} %param.15) | copy-start | bytes 24580
  6.5 612.0 %all-reduce.9.cloned.1.call-start = ((), (), s32[]{:S(2)}) async-start(), calls=%async_computation | async-start | bytes 131072 | tf_op jit(solution)/shard_map/psum | solution.py:148
  7.3 8.4 %collective-permute-start.1 = (f32[1,8,256]{2,1,0:T(8,128)S(1)}, f32[1,8,256]{2,1,0:T(8,128)S(1)}, u32[]{:S(2)}, u32[]{:S(2)}) collective-permute-start(f32[1,8,256]{2,1,0:T(8,128)S(1)} %get-tuple-element.35), channel_id=1, source_target_pairs={{0,16},{16,32},{32,48},{1,17},{17,33},{33,49},{2,18},{18,34},{34,5... | collective-permute-start | bytes 24584 | tf_op jit(solution)/shard_map/ppermute | solution.py:16
  10.7 5.8 collective-permute-start
  16.6 11.5 %collective-permute-start.2 = (f32[10,1,256]{2,1,0:T(1,128)S(1)}, f32[10,1,256]{2,1,0:T(1,128)S(1)}, u32[]{:S(2)}, u32[]{:S(2)}) collective-permute-start(f32[10,1,256]{2,1,0:T(1,128)S(1)} %get-tuple-element.33), channel_id=1, source_target_pairs={{1,0},{2,1},{3,2},{4,3},{5,4},{6,5},{7,6},{8,7},{9,8},{10,9},{11,1... | collective-permute-start | bytes 30728 | tf_op jit(solution)/shard_map/ppermute | solution.py:19
  22.2 5.9 collective-permute-start.3
  29.3 40.8 %copy-start.1 = (f32[8,8,256]{2,1,0:T(8,128)}, f32[8,8,256]{2,1,0:T(8,128)S(1)}, u32[]{:S(2)}) copy-start(f32[8,8,256]{2,1,0:T(8,128)S(1)} %get-tuple-element.7) | copy-start | bytes 196612
  29.3 40.8 %copy-start.3 = (f32[8,8,256]{2,1,0:T(8,128)}, f32[8,8,256]{2,1,0:T(8,128)S(1)}, u32[]{:S(2)}) copy-start(f32[8,8,256]{2,1,0:T(8,128)S(1)} %get-tuple-element.8) | copy-start | bytes 196612
  29.4 40.8 %copy-start.5 = (f32[8,8,256]{2,1,0:T(8,128)}, f32[8,8,256]{2,1,0:T(8,128)S(1)}, u32[]{:S(2)}) copy-start(f32[8,8,256]{2,1,0:T(8,128)S(1)} %get-tuple-element.9) | copy-start | bytes 196612
  29.4 40.8 %copy-start.7 = (f32[8,8,256]{2,1,0:T(8,128)}, f32[8,8,256]{2,1,0:T(8,128)S(1)}, u32[]{:S(2)}) copy-start(f32[8,8,256]{2,1,0:T(8,128)S(1)} %get-tuple-element.10) | copy-start | bytes 196612
  29.4 40.8 %copy-start.9 = (f32[8,8,256]{2,1,0:T(8,128)}, f32[8,8,256]{2,1,0:T(8,128)S(1)}, u32[]{:S(2)}) copy-start(f32[8,8,256]{2,1,0:T(8,128)S(1)} %get-tuple-element.11) | copy-start | bytes 196612
  29.5 6.5 %collective-permute-start.4 = (f32[4,1,8,256]{3,2,1,0:T(8,128)S(1)}, f32[4,1,8,256]{3,2,1,0:T(8,128)S(1)}, u32[]{:S(2)}, u32[]{:S(2)}) collective-permute-start(f32[4,1,8,256]{3,2,1,0:T(8,128)S(1)} %get-tuple-element.31), channel_id=1, source_target_pairs={{16,0},{32,16},{48,32},{17,1},{33,17},{49,33},{18,2},{34,18},{50,3... | collective-permute-start | bytes 98312 | tf_op jit(solution)/shard_map/ppermute | solution.py:19
  30.8 6.8 %collective-permute-start.5 = (f32[4,1,8,256]{3,2,1,0:T(8,128)S(1)}, f32[4,1,8,256]{3,2,1,0:T(8,128)S(1)}, u32[]{:S(2)}, u32[]{:S(2)}) collective-permute-start(f32[4,1,8,256]{3,2,1,0:T(8,128)S(1)} %get-tuple-element.30), channel_id=1, source_target_pairs={{0,16},{16,32},{32,48},{1,17},{17,33},{33,49},{2,18},{18,34},{34,5... | collective-permute-start | bytes 98312 | tf_op jit(solution)/shard_map/ppermute | solution.py:16
  37.6 6.7 %collective-permute-start.6 = (f32[4,10,1,256]{3,2,1,0:T(1,128)S(1)}, f32[4,10,1,256]{3,2,1,0:T(1,128)S(1)}, u32[]{:S(2)}, u32[]{:S(2)}) collective-permute-start(f32[4,10,1,256]{3,2,1,0:T(1,128)S(1)} %get-tuple-element.22), channel_id=1, source_target_pairs={{1,0},{2,1},{3,2},{4,3},{5,4},{6,5},{7,6},{8,7},{9,8},{10,9},{11,1... | collective-permute-start | bytes 122888 | tf_op jit(solution)/shard_map/ppermute | solution.py:19
  41.5 5.9 collective-permute-start.7
  44.3 3.1 copy-start.11
  47.4 0.6 copy-start.12
  49.1 6.2 collective-permute-start.8
  50.4 6.4 %collective-permute-start.9 = (f32[4,1,8,256]{3,2,1,0:T(8,128)S(1)}, f32[4,1,8,256]{3,2,1,0:T(8,128)S(1)}, u32[]{:S(2)}, u32[]{:S(2)}) collective-permute-start(f32[4,1,8,256]{3,2,1,0:T(8,128)S(1)} %get-tuple-element.28), channel_id=1, source_target_pairs={{0,16},{16,32},{32,48},{1,17},{17,33},{33,49},{2,18},{18,34},{34,5... | collective-permute-start | bytes 98312 | tf_op jit(solution)/shard_map/ppermute | solution.py:16
  56.9 8.2 %collective-permute-start.10 = (f32[4,10,1,256]{3,2,1,0:T(1,128)S(1)}, f32[4,10,1,256]{3,2,1,0:T(1,128)S(1)}, u32[]{:S(2)}, u32[]{:S(2)}) collective-permute-start(f32[4,10,1,256]{3,2,1,0:T(1,128)S(1)} %get-tuple-element.20), channel_id=1, source_target_pairs={{1,0},{2,1},{3,2},{4,3},{5,4},{6,5},{7,6},{8,7},{9,8},{10,9},{11,1... | collective-permute-start | bytes 122888 | tf_op jit(solution)/shard_map/ppermute | solution.py:19
  58.8 6.3 %collective-permute-start.11 = (f32[4,10,1,256]{3,2,1,0:T(1,128)S(1)}, f32[4,10,1,256]{3,2,1,0:T(1,128)S(1)}, u32[]{:S(2)}, u32[]{:S(2)}) collective-permute-start(f32[4,10,1,256]{3,2,1,0:T(1,128)S(1)} %get-tuple-element.21), channel_id=1, source_target_pairs={{0,1},{1,2},{2,3},{3,4},{4,5},{5,6},{6,7},{7,8},{8,9},{9,10},{10,1... | collective-permute-start | bytes 122888 | tf_op jit(solution)/shard_map/ppermute | solution.py:16
  379.4 114.3 %copy-start.2 = (f32[8,8,256]{2,1,0:T(8,128)S(1)}, f32[8,8,256]{2,1,0:T(8,128)}, u32[]{:S(2)}) copy-start(f32[8,8,256]{2,1,0:T(8,128)} %copy-done.1) | copy-start | bytes 196612
  379.4 114.3 %copy-start.4 = (f32[8,8,256]{2,1,0:T(8,128)S(1)}, f32[8,8,256]{2,1,0:T(8,128)}, u32[]{:S(2)}) copy-start(f32[8,8,256]{2,1,0:T(8,128)} %copy-done.3) | copy-start | bytes 196612
  379.4 114.3 %copy-start.6 = (f32[8,8,256]{2,1,0:T(8,128)S(1)}, f32[8,8,256]{2,1,0:T(8,128)}, u32[]{:S(2)}) copy-start(f32[8,8,256]{2,1,0:T(8,128)} %copy-done.5) | copy-start | bytes 196612
  379.4 114.3 %copy-start.8 = (f32[8,8,256]{2,1,0:T(8,128)S(1)}, f32[8,8,256]{2,1,0:T(8,128)}, u32[]{:S(2)}) copy-start(f32[8,8,256]{2,1,0:T(8,128)} %copy-done.7) | copy-start | bytes 196612
  379.4 114.3 %copy-start.10 = (f32[8,8,256]{2,1,0:T(8,128)S(1)}, f32[8,8,256]{2,1,0:T(8,128)}, u32[]{:S(2)}) copy-start(f32[8,8,256]{2,1,0:T(8,128)} %copy-done.9) | copy-start | bytes 196612
  476.3 5.9 collective-permute-start.12
  477.6 6.1 collective-permute-start.13
  483.8 5.9 collective-permute-start.14
  487.8 5.9 collective-permute-start.15
  493.9 6.2 collective-permute-start.16
  495.2 6.4 %collective-permute-start.17 = (f32[4,1,8,256]{3,2,1,0:T(8,128)S(1)}, f32[4,1,8,256]{3,2,1,0:T(8,128)S(1)}, u32[]{:S(2)}, u32[]{:S(2)}) collective-permute-start(f32[4,1,8,256]{3,2,1,0:T(8,128)S(1)} %get-tuple-element.24), channel_id=1, source_target_pairs={{0,16},{16,32},{32,48},{1,17},{17,33},{33,49},{2,18},{18,34},{34,5... | collective-permute-start | bytes 98312 | tf_op jit(solution)/shard_map/ppermute | solution.py:16
  501.7 5.9 collective-permute-start.18
  503.7 5.9 collective-permute-start.19
  509.8 6.5 %collective-permute-start.20 = (f32[8,1,8,256]{3,2,1,0:T(8,128)S(1)}, f32[8,1,8,256]{3,2,1,0:T(8,128)S(1)}, u32[]{:S(2)}, u32[]{:S(2)}) collective-permute-start(f32[8,1,8,256]{3,2,1,0:T(8,128)S(1)} %get-tuple-element.15), channel_id=1, source_target_pairs={{16,0},{32,16},{48,32},{17,1},{33,17},{49,33},{18,2},{34,18},{50,3... | collective-permute-start | bytes 196616 | tf_op jit(solution)/shard_map/ppermute | solution.py:19
  511.1 6.7 %collective-permute-start.21 = (f32[8,1,8,256]{3,2,1,0:T(8,128)S(1)}, f32[8,1,8,256]{3,2,1,0:T(8,128)S(1)}, u32[]{:S(2)}, u32[]{:S(2)}) collective-permute-start(f32[8,1,8,256]{3,2,1,0:T(8,128)S(1)} %get-tuple-element.14), channel_id=1, source_target_pairs={{0,16},{16,32},{32,48},{1,17},{17,33},{33,49},{2,18},{18,34},{34,5... | collective-permute-start | bytes 196616 | tf_op jit(solution)/shard_map/ppermute | solution.py:16
  518.0 6.3 %collective-permute-start.22 = (f32[8,10,1,256]{3,2,1,0:T(1,128)S(1)}, f32[8,10,1,256]{3,2,1,0:T(1,128)S(1)}, u32[]{:S(2)}, u32[]{:S(2)}) collective-permute-start(f32[8,10,1,256]{3,2,1,0:T(1,128)S(1)} %get-tuple-element.12), channel_id=1, source_target_pairs={{1,0},{2,1},{3,2},{4,3},{5,4},{6,5},{7,6},{8,7},{9,8},{10,9},{11,1... | collective-permute-start | bytes 245768 | tf_op jit(solution)/shard_map/ppermute | solution.py:19
  519.9 6.3 %collective-permute-start.23 = (f32[8,10,1,256]{3,2,1,0:T(1,128)S(1)}, f32[8,10,1,256]{3,2,1,0:T(1,128)S(1)}, u32[]{:S(2)}, u32[]{:S(2)}) collective-permute-start(f32[8,10,1,256]{3,2,1,0:T(1,128)S(1)} %get-tuple-element.13), channel_id=1, source_target_pairs={{0,1},{1,2},{2,3},{3,4},{4,5},{5,6},{6,7},{7,8},{8,9},{9,10},{10,1... | collective-permute-start | bytes 245768 | tf_op jit(solution)/shard_map/ppermute | solution.py:16
Sparse Core Ops, SparseCore 0:
  527.5 90.9 all-reduce.8
where the time goes:
time: 628 us; the launch traced here: 627 us
  blocking collectives  236 us (38%)
  other arithmetic  117 us (19%)
  waiting for transfers between devices  111 us (18%)
  local copies, waits for them, and re-layouts  75.6 us (12%)
  starting transfers between devices  73 us (12%)
  between operations  14 us (2%)
    psum x1, blocking collectives, per_sweep_terms(): lax.psum(jnp.sum(residual * residual, axis=1), ('bx', 'by')) / well_count  236 us
    scatter-add x1, other arithmetic, per_sweep_terms(): jnp.zeros((tests_here, cell_count), jnp.float32)  91.6 us
    psum x1, waiting for transfers between devices, local(): grand_total = lax.psum(local_sum, 'test')  91.2 us
    gather x1, local copies, waits for them, and re-layouts, per_sweep_terms(): heads_field.reshape(tests_here, cell_count)[:, screen_cells]  58.2 us
    ppermute x12, starting transfers between devices, with_halo(): lax.ppermute(lax.slice_in_dim(block, block.shape[dim] - width, None, axis...  45.9 us
    ppermute x12, starting transfers between devices, with_halo(): lax.ppermute(lax.slice_in_dim(block, 0, width, axis=dim), axis, backward)  27.1 us
    ppermute x12, waiting for transfers between devices, with_halo(): lax.ppermute(lax.slice_in_dim(block, block.shape[dim] - width, None, axis...  18.8 us
    reduce_sum x1, other arithmetic, per_sweep_terms(): jnp.mean(heads_field.reshape(tests_here, cell_count)[:, screen_cells], ax...  13 us
  transfers between devices with their start and end apart: 25, of which 12 were waited for; matrix products, arithmetic and copies ran while one was open for 2% of the time, Pallas kernels for 0%

commit v1 on v0

--- a/solution.py
+++ b/solution.py
@@ -2,10 +2,17 @@
 import jax.numpy as jnp
 from jax import lax
 from jax.sharding import PartitionSpec as P
+from jax.lax import psum
 
 SWEEPS = 3
 SCREEN = 8
 epsilon = 1e-06
+
+
+def extend_patches(a0, axis_key, named_axis):
+    for dev_j in (axis_key, named_axis):
+        a0 = psum(a0, axis_name=dev_j)
+    return a0
 
 
 def with_halo(block, sides, width):
@@ -99,7 +106,7 @@
     well_heads = jnp.mean(heads_field.reshape(tests_here, cell_count)[:, screen_cells], axis=2)
     residual = jnp.where(owned_here[None, :], well_heads - observed, 0.0)
     well_count = residual.shape[1]
-    misfit = lax.psum(jnp.sum(residual * residual, axis=1), ("bx", "by")) / well_count + epsilon
+    misfit = extend_patches(jnp.sum(residual * residual, axis=1), "by", "bx") / well_count + epsilon
     weights = residual / misfit[:, None]
     values = jnp.broadcast_to(weights[:, :, None], (tests_here, well_count, SCREEN)).reshape(
         tests_here, -1

time: 628 us -> 483 us (0.77)
  blocking collectives: 236 us -> 78.2 us
  waiting for transfers between devices: 111 us -> 123 us
    psum x1 -> x2, blocking collectives: 236 us -> 78.2 us  [extend_patches(): a0 = psum(a0, axis_name=dev_j)]
    psum x1, waiting for transfers between devices: 91.2 us -> 103 us  [local(): grand_total = lax.psum(local_sum, 'test')]
  transfers between devices with their start and end apart: 25 -> 25, of which waited for: 12 -> 13; matrix products, arithmetic and copies ran while one was open for 2% -> 2% of each run, Pallas kernels for 0% -> 0%
where the time goes in v1:
time: 483 us; the launch traced here: 481 us
  waiting for transfers between devices  123 us (25%)
  other arithmetic  118 us (24%)
  blocking collectives  78.2 us (16%)
  local copies, waits for them, and re-layouts  74.9 us (16%)
  starting transfers between devices  72.9 us (15%)
  between operations  14 us (3%)
    psum x1, waiting for transfers between devices, local(): grand_total = lax.psum(local_sum, 'test')  103 us
    scatter-add x1, other arithmetic, per_sweep_terms(): jnp.zeros((tests_here, cell_count), jnp.float32)  91.6 us
    psum x2, blocking collectives, extend_patches(): a0 = psum(a0, axis_name=dev_j)  78.2 us
    gather x1, local copies, waits for them, and re-layouts, per_sweep_terms(): heads_field.reshape(tests_here, cell_count)[:, screen_cells]  58.1 us
    ppermute x12, starting transfers between devices, with_halo(): lax.ppermute(lax.slice_in_dim(block, block.shape[dim] - width, None, axis...  46 us
    ppermute x12, starting transfers between devices, with_halo(): lax.ppermute(lax.slice_in_dim(block, 0, width, axis=dim), axis, backward)  27 us
    ppermute x12, waiting for transfers between devices, with_halo(): lax.ppermute(lax.slice_in_dim(block, block.shape[dim] - width, None, axis...  19.9 us
    reduce_sum x1, other arithmetic, per_sweep_terms(): jnp.mean(heads_field.reshape(tests_here, cell_count)[:, screen_cells], ax...  13 us
  transfers between devices with their start and end apart: 25, of which 13 were waited for; matrix products, arithmetic and copies ran while one was open for 2% of the time, Pallas kernels for 0%

profile of v1, /device:TPU:2, one launch (start us, length us, event | category | flops | bytes accessed | tf_op | source)
XLA Modules:
  0.0 481.5 jit_solution(7885473183945239675)
XLA Ops:
  7.3 3.5 collective-permute-start.1
  10.8 1.3 collective-permute-start
  14.4 1.3 gather_fusion.1
  16.6 5.6 %collective-permute-start.2 = (f32[10,1,256]{2,1,0:T(1,128)S(1)}, f32[10,1,256]{2,1,0:T(1,128)S(1)}, u32[]{:S(2)}, u32[]{:S(2)}) collective-permute-start(f32[10,1,256]{2,1,0:T(1,128)S(1)} %get-tuple-element.33), channel_id=1, source_target_pairs={{1,0},{2,1},{3,2},{4,3},{5,4},{6,5},{7,6},{8,7},{9,8},{10,9},{11,1... | collective-permute-start | bytes 30728 | tf_op jit(solution)/shard_map/ppermute | solution.py:26
  22.2 1.9 collective-permute-start.3
  26.0 2.1 scatter_fusion
  28.1 1.2 add_add_fusion
  29.5 1.3 collective-permute-start.4
  30.8 5.2 %collective-permute-start.5 = (f32[4,1,8,256]{3,2,1,0:T(8,128)S(1)}, f32[4,1,8,256]{3,2,1,0:T(8,128)S(1)}, u32[]{:S(2)}, u32[]{:S(2)}) collective-permute-start(f32[4,1,8,256]{3,2,1,0:T(8,128)S(1)} %get-tuple-element.30), channel_id=1, source_target_pairs={{0,16},{16,32},{32,48},{1,17},{17,33},{33,49},{2,18},{18,34},{34,5... | collective-permute-start | bytes 98312 | tf_op jit(solution)/shard_map/ppermute | solution.py:23
  36.0 1.6 collective-permute-done.5
  37.6 3.9 collective-permute-start.6
  41.5 1.9 collective-permute-start.7
  44.3 3.1 collective-permute-done.7
  47.7 1.3 collective-permute-start.8
  49.0 4.9 %collective-permute-start.9 = (f32[4,1,8,256]{3,2,1,0:T(8,128)S(1)}, f32[4,1,8,256]{3,2,1,0:T(8,128)S(1)}, u32[]{:S(2)}, u32[]{:S(2)}) collective-permute-start(f32[4,1,8,256]{3,2,1,0:T(8,128)S(1)} %get-tuple-element.28), channel_id=1, source_target_pairs={{0,16},{16,32},{32,48},{1,17},{17,33},{33,49},{2,18},{18,34},{34,5... | collective-permute-start | bytes 98312 | tf_op jit(solution)/shard_map/ppermute | solution.py:23
  53.9 1.5 collective-permute-done.9
  55.5 1.9 collective-permute-start.10
  57.4 4.6 collective-permute-start.11
  62.5 1.2 collective-permute-done.11
  63.7 1.3 fusion.15
  64.9 4.7 copy.20
  69.7 58.1 %gather_fusion.2 = f32[16384,4]{1,0:T(8,128)} fusion(f32[4,16384]{0,1:T(8,128)} %bitcast.34, s32[16384]{0:T(1024)S(1)} %broadcast_clamp_fusion), kind=kCustom, calls=%fused_computation.2 | custom fusion | bytes 589824 | tf_op jit(solution)/shard_map/gather | solution.py:106
  127.8 13.0 %bitcast_reduce_fusion = f32[2048,4]{1,0:T(8,128)S(1)} fusion(f32[16384,4]{1,0:T(8,128)} %gather_fusion.2), kind=kLoop, calls=%fused_computation.7 | loop fusion | flops 57344 | bytes 294912 | tf_op jit(solution)/shard_map/reduce_sum | solution.py:106
  142.4 65.4 %psum.21 = f32[4]{0:T(128)S(1)} all-reduce(f32[4]{0:T(128)S(1)} %multiply_reduce_fusion), channel_id=1, replica_groups=mesh['test'=8,'bx'=4,'by'=16] {'by'}, use_global_device_ids=true, to_apply=%region_3.4 | all-reduce | flops 4 | bytes 32 | tf_op jit(solution)/shard_map/psum | solution.py:14
  207.9 1.5 compare_select_fusion.1
  209.4 12.8 %psum.22 = f32[4]{0:T(128)S(1)} all-reduce(f32[4]{0:T(128)S(1)} %psum.21), channel_id=1, replica_groups=mesh['test'=8,'bx'=4,'by'=16] {'bx'}, use_global_device_ids=true, to_apply=%region_4.5 | all-reduce | flops 4 | bytes 32 | tf_op jit(solution)/shard_map/psum | solution.py:14
  222.7 91.6 %scatter_custom_fusion.1 = f32[4,16384]{0,1:T(8,128)} fusion(s32[16384]{0:T(1024)} %bitcast.41, f32[4,2048]{0,1:T(8,128)S(1)} %broadcast_divide_fusion, f32[]{:T(128)} %constant.27.clone.1), kind=kCustom, calls=%fused_computation.5 | custom fusion | flops 65536 | bytes 295424 | tf_op jit(solution)/shard_map/scatter-add | solution.py:115
  314.2 5.2 %copy.24 = f32[4,8,8,256]{3,2,1,0:T(8,128)S(1)} copy(f32[4,8,8,256]{0,3,2,1:T(8,128)} %bitcast.38) | data formatting | bytes 524288 | tf_op jit(solution)/shard_map/reshape | solution.py:118
  319.5 1.3 collective-permute-start.12
  320.8 4.5 collective-permute-start.13
  325.4 1.6 collective-permute-done.13
  327.0 3.9 collective-permute-start.14
  330.9 1.9 collective-permute-start.15
  332.9 3.9 collective-permute-done.15
  337.1 1.3 collective-permute-start.16
  338.4 4.9 %collective-permute-start.17 = (f32[4,1,8,256]{3,2,1,0:T(8,128)S(1)}, f32[4,1,8,256]{3,2,1,0:T(8,128)S(1)}, u32[]{:S(2)}, u32[]{:S(2)}) collective-permute-start(f32[4,1,8,256]{3,2,1,0:T(8,128)S(1)} %get-tuple-element.24), channel_id=1, source_target_pairs={{0,16},{16,32},{32,48},{1,17},{17,33},{33,49},{2,18},{18,34},{34,5... | collective-permute-start | bytes 98312 | tf_op jit(solution)/shard_map/ppermute | solution.py:23
  343.3 1.6 collective-permute-done.17
  344.9 1.9 collective-permute-start.18
  346.9 3.9 collective-permute-start.19
  350.8 1.9 collective-permute-done.19
  353.0 1.3 collective-permute-start.20
  354.3 4.9 %collective-permute-start.21 = (f32[8,1,8,256]{3,2,1,0:T(8,128)S(1)}, f32[8,1,8,256]{3,2,1,0:T(8,128)S(1)}, u32[]{:S(2)}, u32[]{:S(2)}) collective-permute-start(f32[8,1,8,256]{3,2,1,0:T(8,128)S(1)} %get-tuple-element.14), channel_id=1, source_target_pairs={{0,16},{16,32},{32,48},{1,17},{17,33},{33,49},{2,18},{18,34},{34,5... | collective-permute-start | bytes 196616 | tf_op jit(solution)/shard_map/ppermute | solution.py:23
  359.5 1.6 collective-permute-done.21
  361.2 1.9 collective-permute-start.22
  363.1 3.9 collective-permute-start.23
  367.5 1.9 collective-permute-done.23
  370.6 102.6 %all-reduce.9.cloned.1.call-done = f32[8,8,256]{2,1,0:T(8,128)} async-done(((f32[8,8,256]{2,1,0:T(8,128)}), f32[8,8,256]{2,1,0:T(8,128)}) %all-reduce.9.cloned.1.call-update) | async-done | bytes 65552 | tf_op jit(solution)/shard_map/psum | solution.py:155
  473.2 1.4 dynamic-slice_multiply_fusion
  (82 shorter events, 12.2 us)
Async XLA Ops:
  6.5 55.5 %copy-start = (s32[2048]{0:T(1024)S(1)}, s32[2048]{0:T(1024)}, u32[]{:S(2)}) copy-start(s32[2048]{0:T(1024)} %param.15) | copy-start | bytes 24580
  6.5 55.6 %copy-start.11 = (f32[4,2048]{1,0:T(4,128)S(1)}, f32[4,2048]{1,0:T(4,128)}, u32[]{:S(2)}) copy-start(f32[4,2048]{1,0:T(4,128)} %param.14) | copy-start | bytes 98308
  6.5 466.6 %all-reduce.9.cloned.1.call-start = ((), (), s32[]{:S(2)}) async-start(), calls=%async_computation | async-start | bytes 131072 | tf_op jit(solution)/shard_map/psum | solution.py:155
  7.3 8.4 %collective-permute-start.1 = (f32[1,8,256]{2,1,0:T(8,128)S(1)}, f32[1,8,256]{2,1,0:T(8,128)S(1)}, u32[]{:S(2)}, u32[]{:S(2)}) collective-permute-start(f32[1,8,256]{2,1,0:T(8,128)S(1)} %get-tuple-element.35), channel_id=1, source_target_pairs={{0,16},{16,32},{32,48},{1,17},{17,33},{33,49},{2,18},{18,34},{34,5... | collective-permute-start | bytes 24584 | tf_op jit(solution)/shard_map/ppermute | solution.py:23
  10.8 5.8 %collective-permute-start = (f32[1,8,256]{2,1,0:T(8,128)S(1)}, f32[1,8,256]{2,1,0:T(8,128)S(1)}, u32[]{:S(2)}, u32[]{:S(2)}) collective-permute-start(f32[1,8,256]{2,1,0:T(8,128)S(1)} %get-tuple-element.34), channel_id=1, source_target_pairs={{16,0},{32,16},{48,32},{17,1},{33,17},{49,33},{18,2},{34,18},{50,3... | collective-permute-start | bytes 24584 | tf_op jit(solution)/shard_map/ppermute | solution.py:26
  16.6 11.5 %collective-permute-start.2 = (f32[10,1,256]{2,1,0:T(1,128)S(1)}, f32[10,1,256]{2,1,0:T(1,128)S(1)}, u32[]{:S(2)}, u32[]{:S(2)}) collective-permute-start(f32[10,1,256]{2,1,0:T(1,128)S(1)} %get-tuple-element.33), channel_id=1, source_target_pairs={{1,0},{2,1},{3,2},{4,3},{5,4},{6,5},{7,6},{8,7},{9,8},{10,9},{11,1... | collective-permute-start | bytes 30728 | tf_op jit(solution)/shard_map/ppermute | solution.py:26
  22.2 5.9 %collective-permute-start.3 = (f32[10,1,256]{2,1,0:T(1,128)S(1)}, f32[10,1,256]{2,1,0:T(1,128)S(1)}, u32[]{:S(2)}, u32[]{:S(2)}) collective-permute-start(f32[10,1,256]{2,1,0:T(1,128)S(1)} %get-tuple-element.32), channel_id=1, source_target_pairs={{0,1},{1,2},{2,3},{3,4},{4,5},{5,6},{6,7},{7,8},{8,9},{9,10},{10,1... | collective-permute-start | bytes 30728 | tf_op jit(solution)/shard_map/ppermute | solution.py:23
  29.3 32.7 %copy-start.1 = (f32[8,8,256]{2,1,0:T(8,128)}, f32[8,8,256]{2,1,0:T(8,128)S(1)}, u32[]{:S(2)}) copy-start(f32[8,8,256]{2,1,0:T(8,128)S(1)} %get-tuple-element.7) | copy-start | bytes 196612
  29.4 32.7 %copy-start.3 = (f32[8,8,256]{2,1,0:T(8,128)}, f32[8,8,256]{2,1,0:T(8,128)S(1)}, u32[]{:S(2)}) copy-start(f32[8,8,256]{2,1,0:T(8,128)S(1)} %get-tuple-element.8) | copy-start | bytes 196612
  29.4 32.7 %copy-start.5 = (f32[8,8,256]{2,1,0:T(8,128)}, f32[8,8,256]{2,1,0:T(8,128)S(1)}, u32[]{:S(2)}) copy-start(f32[8,8,256]{2,1,0:T(8,128)S(1)} %get-tuple-element.9) | copy-start | bytes 196612
  29.4 32.7 %copy-start.7 = (f32[8,8,256]{2,1,0:T(8,128)}, f32[8,8,256]{2,1,0:T(8,128)S(1)}, u32[]{:S(2)}) copy-start(f32[8,8,256]{2,1,0:T(8,128)S(1)} %get-tuple-element.10) | copy-start | bytes 196612
  29.4 32.7 %copy-start.9 = (f32[8,8,256]{2,1,0:T(8,128)}, f32[8,8,256]{2,1,0:T(8,128)S(1)}, u32[]{:S(2)}) copy-start(f32[8,8,256]{2,1,0:T(8,128)S(1)} %get-tuple-element.11) | copy-start | bytes 196612
  29.5 6.5 %collective-permute-start.4 = (f32[4,1,8,256]{3,2,1,0:T(8,128)S(1)}, f32[4,1,8,256]{3,2,1,0:T(8,128)S(1)}, u32[]{:S(2)}, u32[]{:S(2)}) collective-permute-start(f32[4,1,8,256]{3,2,1,0:T(8,128)S(1)} %get-tuple-element.31), channel_id=1, source_target_pairs={{16,0},{32,16},{48,32},{17,1},{33,17},{49,33},{18,2},{34,18},{50,3... | collective-permute-start | bytes 98312 | tf_op jit(solution)/shard_map/ppermute | solution.py:26
  30.8 6.8 %collective-permute-start.5 = (f32[4,1,8,256]{3,2,1,0:T(8,128)S(1)}, f32[4,1,8,256]{3,2,1,0:T(8,128)S(1)}, u32[]{:S(2)}, u32[]{:S(2)}) collective-permute-start(f32[4,1,8,256]{3,2,1,0:T(8,128)S(1)} %get-tuple-element.30), channel_id=1, source_target_pairs={{0,16},{16,32},{32,48},{1,17},{17,33},{33,49},{2,18},{18,34},{34,5... | collective-permute-start | bytes 98312 | tf_op jit(solution)/shard_map/ppermute | solution.py:23
  37.6 6.7 %collective-permute-start.6 = (f32[4,10,1,256]{3,2,1,0:T(1,128)S(1)}, f32[4,10,1,256]{3,2,1,0:T(1,128)S(1)}, u32[]{:S(2)}, u32[]{:S(2)}) collective-permute-start(f32[4,10,1,256]{3,2,1,0:T(1,128)S(1)} %get-tuple-element.22), channel_id=1, source_target_pairs={{1,0},{2,1},{3,2},{4,3},{5,4},{6,5},{7,6},{8,7},{9,8},{10,9},{11,1... | collective-permute-start | bytes 122888 | tf_op jit(solution)/shard_map/ppermute | solution.py:26
  41.5 5.9 %collective-permute-start.7 = (f32[4,10,1,256]{3,2,1,0:T(1,128)S(1)}, f32[4,10,1,256]{3,2,1,0:T(1,128)S(1)}, u32[]{:S(2)}, u32[]{:S(2)}) collective-permute-start(f32[4,10,1,256]{3,2,1,0:T(1,128)S(1)} %get-tuple-element.23), channel_id=1, source_target_pairs={{0,1},{1,2},{2,3},{3,4},{4,5},{5,6},{6,7},{7,8},{8,9},{9,10},{10,1... | collective-permute-start | bytes 122888 | tf_op jit(solution)/shard_map/ppermute | solution.py:23
  47.7 6.2 %collective-permute-start.8 = (f32[4,1,8,256]{3,2,1,0:T(8,128)S(1)}, f32[4,1,8,256]{3,2,1,0:T(8,128)S(1)}, u32[]{:S(2)}, u32[]{:S(2)}) collective-permute-start(f32[4,1,8,256]{3,2,1,0:T(8,128)S(1)} %get-tuple-element.29), channel_id=1, source_target_pairs={{16,0},{32,16},{48,32},{17,1},{33,17},{49,33},{18,2},{34,18},{50,3... | collective-permute-start | bytes 98312 | tf_op jit(solution)/shard_map/ppermute | solution.py:26
  49.0 6.4 %collective-permute-start.9 = (f32[4,1,8,256]{3,2,1,0:T(8,128)S(1)}, f32[4,1,8,256]{3,2,1,0:T(8,128)S(1)}, u32[]{:S(2)}, u32[]{:S(2)}) collective-permute-start(f32[4,1,8,256]{3,2,1,0:T(8,128)S(1)} %get-tuple-element.28), channel_id=1, source_target_pairs={{0,16},{16,32},{32,48},{1,17},{17,33},{33,49},{2,18},{18,34},{34,5... | collective-permute-start | bytes 98312 | tf_op jit(solution)/shard_map/ppermute | solution.py:23
  55.5 7.0 %collective-permute-start.10 = (f32[4,10,1,256]{3,2,1,0:T(1,128)S(1)}, f32[4,10,1,256]{3,2,1,0:T(1,128)S(1)}, u32[]{:S(2)}, u32[]{:S(2)}) collective-permute-start(f32[4,10,1,256]{3,2,1,0:T(1,128)S(1)} %get-tuple-element.20), channel_id=1, source_target_pairs={{1,0},{2,1},{3,2},{4,3},{5,4},{6,5},{7,6},{8,7},{9,8},{10,9},{11,1... | collective-permute-start | bytes 122888 | tf_op jit(solution)/shard_map/ppermute | solution.py:26
  57.4 6.2 %collective-permute-start.11 = (f32[4,10,1,256]{3,2,1,0:T(1,128)S(1)}, f32[4,10,1,256]{3,2,1,0:T(1,128)S(1)}, u32[]{:S(2)}, u32[]{:S(2)}) collective-permute-start(f32[4,10,1,256]{3,2,1,0:T(1,128)S(1)} %get-tuple-element.21), channel_id=1, source_target_pairs={{0,1},{1,2},{2,3},{3,4},{4,5},{5,6},{6,7},{7,8},{8,9},{9,10},{10,1... | collective-permute-start | bytes 122888 | tf_op jit(solution)/shard_map/ppermute | solution.py:23
  222.6 114.2 %copy-start.2 = (f32[8,8,256]{2,1,0:T(8,128)S(1)}, f32[8,8,256]{2,1,0:T(8,128)}, u32[]{:S(2)}) copy-start(f32[8,8,256]{2,1,0:T(8,128)} %copy-done.1) | copy-start | bytes 196612
  222.6 114.2 %copy-start.4 = (f32[8,8,256]{2,1,0:T(8,128)S(1)}, f32[8,8,256]{2,1,0:T(8,128)}, u32[]{:S(2)}) copy-start(f32[8,8,256]{2,1,0:T(8,128)} %copy-done.3) | copy-start | bytes 196612
  222.6 114.2 %copy-start.6 = (f32[8,8,256]{2,1,0:T(8,128)S(1)}, f32[8,8,256]{2,1,0:T(8,128)}, u32[]{:S(2)}) copy-start(f32[8,8,256]{2,1,0:T(8,128)} %copy-done.5) | copy-start | bytes 196612
  222.6 114.2 %copy-start.8 = (f32[8,8,256]{2,1,0:T(8,128)S(1)}, f32[8,8,256]{2,1,0:T(8,128)}, u32[]{:S(2)}) copy-start(f32[8,8,256]{2,1,0:T(8,128)} %copy-done.7) | copy-start | bytes 196612
  222.7 114.2 %copy-start.10 = (f32[8,8,256]{2,1,0:T(8,128)S(1)}, f32[8,8,256]{2,1,0:T(8,128)}, u32[]{:S(2)}) copy-start(f32[8,8,256]{2,1,0:T(8,128)} %copy-done.9) | copy-start | bytes 196612
  319.5 5.9 %collective-permute-start.12 = (f32[4,1,8,256]{3,2,1,0:T(8,128)S(1)}, f32[4,1,8,256]{3,2,1,0:T(8,128)S(1)}, u32[]{:S(2)}, u32[]{:S(2)}) collective-permute-start(f32[4,1,8,256]{3,2,1,0:T(8,128)S(1)} %get-tuple-element.27), channel_id=1, source_target_pairs={{16,0},{32,16},{48,32},{17,1},{33,17},{49,33},{18,2},{34,18},{50,3... | collective-permute-start | bytes 98312 | tf_op jit(solution)/shard_map/ppermute | solution.py:26
  320.8 6.1 %collective-permute-start.13 = (f32[4,1,8,256]{3,2,1,0:T(8,128)S(1)}, f32[4,1,8,256]{3,2,1,0:T(8,128)S(1)}, u32[]{:S(2)}, u32[]{:S(2)}) collective-permute-start(f32[4,1,8,256]{3,2,1,0:T(8,128)S(1)} %get-tuple-element.26), channel_id=1, source_target_pairs={{0,16},{16,32},{32,48},{1,17},{17,33},{33,49},{2,18},{18,34},{34,5... | collective-permute-start | bytes 98312 | tf_op jit(solution)/shard_map/ppermute | solution.py:23
  327.0 5.9 %collective-permute-start.14 = (f32[4,10,1,256]{3,2,1,0:T(1,128)S(1)}, f32[4,10,1,256]{3,2,1,0:T(1,128)S(1)}, u32[]{:S(2)}, u32[]{:S(2)}) collective-permute-start(f32[4,10,1,256]{3,2,1,0:T(1,128)S(1)} %get-tuple-element.18), channel_id=1, source_target_pairs={{1,0},{2,1},{3,2},{4,3},{5,4},{6,5},{7,6},{8,7},{9,8},{10,9},{11,1... | collective-permute-start | bytes 122888 | tf_op jit(solution)/shard_map/ppermute | solution.py:26
  330.9 5.9 %collective-permute-start.15 = (f32[4,10,1,256]{3,2,1,0:T(1,128)S(1)}, f32[4,10,1,256]{3,2,1,0:T(1,128)S(1)}, u32[]{:S(2)}, u32[]{:S(2)}) collective-permute-start(f32[4,10,1,256]{3,2,1,0:T(1,128)S(1)} %get-tuple-element.19), channel_id=1, source_target_pairs={{0,1},{1,2},{2,3},{3,4},{4,5},{5,6},{6,7},{7,8},{8,9},{9,10},{10,1... | collective-permute-start | bytes 122888 | tf_op jit(solution)/shard_map/ppermute | solution.py:23
  337.1 6.2 %collective-permute-start.16 = (f32[4,1,8,256]{3,2,1,0:T(8,128)S(1)}, f32[4,1,8,256]{3,2,1,0:T(8,128)S(1)}, u32[]{:S(2)}, u32[]{:S(2)}) collective-permute-start(f32[4,1,8,256]{3,2,1,0:T(8,128)S(1)} %get-tuple-element.25), channel_id=1, source_target_pairs={{16,0},{32,16},{48,32},{17,1},{33,17},{49,33},{18,2},{34,18},{50,3... | collective-permute-start | bytes 98312 | tf_op jit(solution)/shard_map/ppermute | solution.py:26
  338.4 6.4 %collective-permute-start.17 = (f32[4,1,8,256]{3,2,1,0:T(8,128)S(1)}, f32[4,1,8,256]{3,2,1,0:T(8,128)S(1)}, u32[]{:S(2)}, u32[]{:S(2)}) collective-permute-start(f32[4,1,8,256]{3,2,1,0:T(8,128)S(1)} %get-tuple-element.24), channel_id=1, source_target_pairs={{0,16},{16,32},{32,48},{1,17},{17,33},{33,49},{2,18},{18,34},{34,5... | collective-permute-start | bytes 98312 | tf_op jit(solution)/shard_map/ppermute | solution.py:23
  344.9 5.9 %collective-permute-start.18 = (f32[4,10,1,256]{3,2,1,0:T(1,128)S(1)}, f32[4,10,1,256]{3,2,1,0:T(1,128)S(1)}, u32[]{:S(2)}, u32[]{:S(2)}) collective-permute-start(f32[4,10,1,256]{3,2,1,0:T(1,128)S(1)} %get-tuple-element.16), channel_id=1, source_target_pairs={{1,0},{2,1},{3,2},{4,3},{5,4},{6,5},{7,6},{8,7},{9,8},{10,9},{11,1... | collective-permute-start | bytes 122888 | tf_op jit(solution)/shard_map/ppermute | solution.py:26
  346.9 5.9 %collective-permute-start.19 = (f32[4,10,1,256]{3,2,1,0:T(1,128)S(1)}, f32[4,10,1,256]{3,2,1,0:T(1,128)S(1)}, u32[]{:S(2)}, u32[]{:S(2)}) collective-permute-start(f32[4,10,1,256]{3,2,1,0:T(1,128)S(1)} %get-tuple-element.17), channel_id=1, source_target_pairs={{0,1},{1,2},{2,3},{3,4},{4,5},{5,6},{6,7},{7,8},{8,9},{9,10},{10,1... | collective-permute-start | bytes 122888 | tf_op jit(solution)/shard_map/ppermute | solution.py:23
  353.0 6.5 %collective-permute-start.20 = (f32[8,1,8,256]{3,2,1,0:T(8,128)S(1)}, f32[8,1,8,256]{3,2,1,0:T(8,128)S(1)}, u32[]{:S(2)}, u32[]{:S(2)}) collective-permute-start(f32[8,1,8,256]{3,2,1,0:T(8,128)S(1)} %get-tuple-element.15), channel_id=1, source_target_pairs={{16,0},{32,16},{48,32},{17,1},{33,17},{49,33},{18,2},{34,18},{50,3... | collective-permute-start | bytes 196616 | tf_op jit(solution)/shard_map/ppermute | solution.py:26
  354.3 6.7 %collective-permute-start.21 = (f32[8,1,8,256]{3,2,1,0:T(8,128)S(1)}, f32[8,1,8,256]{3,2,1,0:T(8,128)S(1)}, u32[]{:S(2)}, u32[]{:S(2)}) collective-permute-start(f32[8,1,8,256]{3,2,1,0:T(8,128)S(1)} %get-tuple-element.14), channel_id=1, source_target_pairs={{0,16},{16,32},{32,48},{1,17},{17,33},{33,49},{2,18},{18,34},{34,5... | collective-permute-start | bytes 196616 | tf_op jit(solution)/shard_map/ppermute | solution.py:23
  361.2 6.3 %collective-permute-start.22 = (f32[8,10,1,256]{3,2,1,0:T(1,128)S(1)}, f32[8,10,1,256]{3,2,1,0:T(1,128)S(1)}, u32[]{:S(2)}, u32[]{:S(2)}) collective-permute-start(f32[8,10,1,256]{3,2,1,0:T(1,128)S(1)} %get-tuple-element.12), channel_id=1, source_target_pairs={{1,0},{2,1},{3,2},{4,3},{5,4},{6,5},{7,6},{8,7},{9,8},{10,9},{11,1... | collective-permute-start | bytes 245768 | tf_op jit(solution)/shard_map/ppermute | solution.py:26
  363.1 6.3 %collective-permute-start.23 = (f32[8,10,1,256]{3,2,1,0:T(1,128)S(1)}, f32[8,10,1,256]{3,2,1,0:T(1,128)S(1)}, u32[]{:S(2)}, u32[]{:S(2)}) collective-permute-start(f32[8,10,1,256]{3,2,1,0:T(1,128)S(1)} %get-tuple-element.13), channel_id=1, source_target_pairs={{0,1},{1,2},{2,3},{3,4},{4,5},{5,6},{6,7},{7,8},{8,9},{9,10},{10,1... | collective-permute-start | bytes 245768 | tf_op jit(solution)/shard_map/ppermute | solution.py:23
Sparse Core Ops, SparseCore 0:
  370.7 102.4 all-reduce.8
